TPU v7x, 256 devices: a whole 4x4x8 slice. The times are simulated.
256 devices in a mesh: feat: 8 (over y, z_lo), rows: 32 (over x, z_hi, core).
Axes of the slice: x: 4, y: 4, z: 8 (z_hi: 4, z_lo: 2; z = z_hi * 2 + z_lo), core: 2. Of those that a mesh axis runs over, the one named last changes fastest.
Arguments:
- x_vals: bfloat16 [64, 8, 8, 512, 128], P('rows', 'feat'), may hold values from -6 to 6
- x_blocks: int32 [64, 8, 8], P('rows', 'feat'), may hold values from 0 to 195
- y_vals: bfloat16 [32, 8, 8, 512, 128], P('rows', 'feat'), may hold values from -6 to 6
- y_blocks: int32 [32, 8, 8], P('rows', 'feat'), may hold values from 0 to 97
- user_weights: bfloat16 [256, 200704], P('rows', 'feat'), may hold values from -0.0625 to 0.0625
- item_weights: bfloat16 [256, 100352], P('rows', 'feat'), may hold values from -0.0625 to 0.0625
- observed: int32 [64, 32], P('rows'), may hold values 0 or 1
- ratings: bfloat16 [32768, 8, 2048], P('rows', 'feat'), may hold values from -6 to 6
Outputs:
- grad_user: float32 [256, 200704], P('rows', 'feat')
- grad_item: float32 [256, 100352], P('rows', 'feat')
Inputs may be any that keep to these rules, and one draw needn't show every extreme that they name: `x_blocks`: feature block numbers within one shard. `y_blocks`: feature block numbers within one shard.
All inputs are finite; a program needn't handle non-finite values. No bound on the sum of `observed` on one device may be relied on, other than what follows from the above.
Results may differ from a plain program's by a relative error of at most 0.008.
Values may be sent and summed in bfloat16 or wider, within the bound.
A program may use at most 64 MiB of HBM per device.

v0:
```python
import math

import jax
import jax.numpy as jnp
from jax import lax
from jax.sharding import PartitionSpec as P

TILE = 512
FBW = 128
RANK = 256
IBD = 1


def in_order(tiles, dim):
    tiles = jnp.moveaxis(tiles, 0, dim)
    dims = tiles.shape
    return tiles.reshape(*dims[:dim], dims[dim] * dims[dim + 1], *dims[dim + 2 :])


def gather_packed(arrays, axis, dims):
    vector = jnp.concatenate([a.reshape(-1) for a in arrays])
    lines, at, done = (lax.all_gather(vector, axis), 0, [])
    for a, dim in zip(arrays, dims):
        tiles = lines[:, at : at + a.size].reshape(-1, *a.shape)
        done.append(in_order(tiles, dim))
        at += a.size
    return tuple(done)


def split_up(shard, dim, size):
    dims = shard.shape
    tiles = shard.reshape(*dims[:dim], size, dims[dim] // size, *dims[dim + 1 :])
    return jnp.moveaxis(tiles, dim, 0)


def sent_and_summed(shard, axis, dim):
    size = lax.axis_size(axis)
    tiles = lax.all_to_all(split_up(shard, dim, size), axis, 0, 0, tiled=True)
    return jnp.sum(tiles, axis=0)


def sent_to_all(shard, axis):
    copies = jnp.broadcast_to(shard, (lax.axis_size(axis), *shard.shape))
    return lax.all_to_all(copies, axis, split_axis=0, concat_axis=0, tiled=True)


def collect(shard, axis, dim):
    return in_order(sent_to_all(shard, axis), dim)


def sum_at_owner(shard, axis, dim):
    tiles = split_up(shard, dim, lax.axis_size(axis))
    arrived = lax.all_to_all(tiles, axis, split_axis=0, concat_axis=0, tiled=True)
    return arrived.astype(jnp.float32).sum(axis=0)


def lookup(weights, indices):
    rank_part = weights.shape[0]
    blocks_table = weights.reshape(rank_part, -1, FBW)
    picked = jnp.take(blocks_table, indices.reshape(-1), axis=1)
    return picked.reshape(rank_part, indices.shape[0], indices.shape[2], FBW)


def accumulate(returned, indices, weights):
    rank_part = weights.shape[0]
    totals = jnp.zeros((rank_part, weights.shape[1] // FBW, FBW), jnp.float32)
    totals = totals.at[:, indices.reshape(-1)].add(returned.reshape(rank_part, -1, FBW))
    return totals.reshape(rank_part, -1)


def on_device(x_vals, x_blocks, y_vals, y_blocks, user_weights, item_weights, observed, ratings):
    rank_scale = 1.0 / math.sqrt(RANK)
    grad_scale = 1.0 / (TILE * math.sqrt(RANK))
    user_blocks_n = x_vals.shape[0]
    item_blocks_n = y_vals.shape[0]
    user_ids, item_ids = gather_packed((x_blocks, y_blocks), "rows", (0, 0))
    user_ask = lookup(user_weights, user_ids)
    item_ask = lookup(item_weights, item_ids)
    user_cols, item_cols = (
        lax.all_to_all(user_ask, "rows", split_axis=1, concat_axis=0, tiled=True),
        lax.all_to_all(item_ask, "rows", split_axis=1, concat_axis=0, tiled=True),
    )
    user_part = jnp.einsum(
        "bktc,rbkc->btr", x_vals[:, 0], user_cols, preferred_element_type=jnp.float32
    ).reshape(-1, RANK)
    item_part = jnp.einsum(
        "bktc,rbkc->btr", y_vals[:, 0], item_cols, preferred_element_type=jnp.float32
    ).reshape(-1, RANK)
    user_share = sent_and_summed(user_part, "feat", 0).astype(jnp.bfloat16)
    user_proj = collect(user_share, "feat", 0)
    item_share = sent_and_summed(item_part, "feat", 0).astype(jnp.bfloat16)
    item_all = lax.all_gather(item_share, "rows", axis=0, tiled=True)
    columns_n = item_all.shape[0]
    share_n = item_share.shape[0]
    feat_id = lax.axis_index("feat")
    column = jnp.arange(columns_n, dtype=jnp.int32)
    item_group = column // share_n
    within = column % share_n
    block_column = item_group * IBD + (feat_id * share_n + within) // TILE
    onehot = (
        block_column[None, :] == jnp.arange(observed.shape[1], dtype=jnp.int32)[:, None]
    ).astype(jnp.float32)
    tile_mask = jnp.dot(observed.astype(jnp.float32), onehot)
    rating_local = ratings.reshape(user_blocks_n, TILE, columns_n).astype(jnp.float32)
    predicted = (
        jnp.einsum("ur,cr->uc", user_proj, item_all, preferred_element_type=jnp.float32)
        * rank_scale
    )
    residual = tile_mask[:, None, :] * (
        predicted.reshape(user_blocks_n, TILE, columns_n) - rating_local
    )
    residual = residual.reshape(-1, columns_n).astype(jnp.bfloat16)
    grad_part = jnp.dot(residual, item_all, preferred_element_type=jnp.float32) * grad_scale
    grad_share = sent_and_summed(grad_part, "feat", 0).astype(jnp.bfloat16)
    user_grad = collect(grad_share, "feat", 0)
    item_terms = (
        jnp.einsum("uc,ur->cr", residual, user_proj, preferred_element_type=jnp.float32)
        * grad_scale
    )
    item_grad = sum_at_owner(item_terms.astype(jnp.bfloat16), "rows", 0)
    item_grad_group = collect(item_grad.astype(jnp.bfloat16), "feat", 0)
    user_grad_blocks = jnp.einsum(
        "btr,bktc->rbkc",
        user_grad.reshape(user_blocks_n, TILE, RANK),
        x_vals[:, 0],
        preferred_element_type=jnp.float32,
    )
    item_grad_blocks = jnp.einsum(
        "btr,bktc->rbkc",
        item_grad_group.reshape(item_blocks_n, TILE, RANK),
        y_vals[:, 0],
        preferred_element_type=jnp.float32,
    )
    back_user, back_item = (
        lax.all_to_all(
            user_grad_blocks.astype(jnp.bfloat16), "rows", split_axis=0, concat_axis=1, tiled=True
        ).astype(user_grad_blocks.dtype),
        lax.all_to_all(
            item_grad_blocks.astype(jnp.bfloat16), "rows", split_axis=0, concat_axis=1, tiled=True
        ).astype(item_grad_blocks.dtype),
    )
    return (
        accumulate(back_user, user_ids, user_weights),
        accumulate(back_item, item_ids, item_weights),
    )


def solution(mesh):
    return jax.shard_map(
        on_device,
        mesh=mesh,
        in_specs=(
            P("rows", "feat", None, None, None),
            P("rows", "feat", None),
            P("rows", "feat", None, None, None),
            P("rows", "feat", None),
            P("rows", "feat"),
            P("rows", "feat"),
            P("rows", None),
            P("rows", "feat", None),
        ),
        out_specs=(P("rows", "feat"), P("rows", "feat")),
        check_vma=False,
    )
```

profile of v0, /device:TPU:1, one launch (start us, length us, event | category | flops | bytes accessed | tf_op | source)
XLA Modules:
  0.0 358.5 jit_solution(3203809252723157743)
XLA Ops:
  11.9 18.8 %all-reduce = s32[768]{0:T(1024)S(1)} all-reduce(s32[768]{0:T(1024)S(1)} %add_dynamic-update-slice_fusion), channel_id=2, replica_groups=mesh['feat'=8,'rows'=32] {'rows'}, use_global_device_ids=true, to_apply=%add | all-reduce | flops 768 | bytes 6144
  34.2 8.2 %all-to-all-start.3 = ((bf16[8,32,8,128]{3,2,0,1:T(8,128)(2,1)}), bf16[8,32,8,128]{3,2,0,1:T(8,128)(2,1)}, u32[]{:S(2)}, u32[]{:S(2)}) async-start(bf16[8,32,8,128]{3,2,0,1:T(8,128)(2,1)} %copy.36), calls=%async_computation.3 | async-start | bytes 1048576 | tf_op jit(solution)/shard_map/all_to_all | solution.py:81
  45.3 1.9 gather_fusion
  49.2 11.5 %all-to-all-done.3 = bf16[8,32,8,128]{3,2,0,1:T(8,128)(2,1)} async-done(((bf16[8,32,8,128]{3,2,0,1:T(8,128)(2,1)}), bf16[8,32,8,128]{3,2,0,1:T(8,128)(2,1)}, u32[]{:S(2)}, u32[]{:S(2)}) %all-to-all-start.3) | async-done | bytes 524320 | tf_op jit(solution)/shard_map/all_to_all | solution.py:81
  60.7 4.8 %all-to-all-start = ((bf16[8,64,8,128]{3,2,0,1:T(8,128)(2,1)}), bf16[8,64,8,128]{3,2,0,1:T(8,128)(2,1)S(1)}, u32[]{:S(2)}, u32[]{:S(2)}) async-start(bf16[8,64,8,128]{3,2,0,1:T(8,128)(2,1)} %copy_select_fusion), calls=%async_computation | async-start | bytes 2097152 | tf_op jit(solution)/shard_map/all_to_all | solution.py:80
  65.5 2.7 convolution_bitcast_fusion.1
  68.2 26.3 %all-to-all-done = bf16[8,64,8,128]{3,2,0,1:T(8,128)(2,1)S(1)} async-done(((bf16[8,64,8,128]{3,2,0,1:T(8,128)(2,1)}), bf16[8,64,8,128]{3,2,0,1:T(8,128)(2,1)S(1)}, u32[]{:S(2)}, u32[]{:S(2)}) %all-to-all-start) | async-done | bytes 1048608 | tf_op jit(solution)/shard_map/all_to_all | solution.py:80
  94.5 4.2 %all-to-all-start.4 = ((f32[8,64,256]{2,1,0:T(8,128)}), f32[8,64,256]{2,1,0:T(8,128)}, u32[]{:S(2)}, u32[]{:S(2)}) async-start(f32[8,64,256]{2,1,0:T(8,128)} %convolution_bitcast_fusion.1), calls=%async_computation.4 | async-start | bytes 1048576 | tf_op jit(solution)/shard_map/all_to_all | solution.py:38
  100.4 2.5 copy.34
  103.0 4.4 %all-to-all-done.4 = f32[8,64,256]{2,1,0:T(8,128)} async-done(((f32[8,64,256]{2,1,0:T(8,128)}), f32[8,64,256]{2,1,0:T(8,128)}, u32[]{:S(2)}, u32[]{:S(2)}) %all-to-all-start.4) | async-done | bytes 524320 | tf_op jit(solution)/shard_map/all_to_all | solution.py:38
  107.4 3.6 all-to-all-start.1
  112.7 11.6 %all-to-all-done.1 = f32[8,128,256]{2,1,0:T(8,128)S(1)} async-done(((f32[8,128,256]{2,1,0:T(8,128)}), f32[8,128,256]{2,1,0:T(8,128)S(1)}, u32[]{:S(2)}, u32[]{:S(2)}) %all-to-all-start.1) | async-done | bytes 1048608 | tf_op jit(solution)/shard_map/all_to_all | solution.py:38
  125.3 3.5 all-to-all-start.2
  129.0 38.1 %all-gather.3.cloned.1.call-done = bf16[2048,256]{1,0:T(8,128)(2,1)} async-done(((bf16[64,256]{1,0:T(8,128)(2,1)}), bf16[2048,256]{1,0:T(8,128)(2,1)}) %all-gather.3.cloned.1.call-update) | async-done | bytes 1048592 | tf_op jit(solution)/shard_map/all_gather | solution.py:92
  167.1 3.9 %fusion.1 = bf16[1024,2048]{1,0:T(8,128)(2,1)S(1)} fusion(bf16[1024,256]{1,0:T(8,128)(2,1)S(1)} %bitcast.120, bf16[2048,256]{1,0:T(8,128)(2,1)} %all-gather.3.cloned.1.call-done, bf16[1024,1,2048]{2,0,1:T(8,128)(2,1)} %param.15, f32[2,2048]{1,0:T(2,128)S(1)} %convolution_bitcast_fusion), kind=kOutput, calls=%fused_computation.6 | convolution fusion | flops 1084227584 | bytes 9977856 | tf_op jit(solution)/shard_map/ur,cr->uc/dot_general | solution.py:106
  171.0 2.4 fusion.2
  173.5 6.1 %all-to-all-start.8 = ((bf16[32,64,256]{2,1,0:T(8,128)(2,1)}), bf16[32,64,256]{2,1,0:T(8,128)(2,1)S(1)}, u32[]{:S(2)}, u32[]{:S(2)}) async-start(bf16[32,64,256]{2,1,0:T(8,128)(2,1)} %bitcast.129), calls=%async_computation.8 | async-start | bytes 2097152 | tf_op jit(solution)/shard_map/all_to_all | solution.py:53
  179.5 4.7 %convolution_multiply_fusion.1 = f32[1024,256]{1,0:T(8,128)} fusion(bf16[1024,2048]{1,0:T(8,128)(2,1)} %copy-done.3, bf16[2048,256]{1,0:T(8,128)(2,1)} %all-gather.3.cloned.1.call-done), kind=kOutput, calls=%fused_computation.18 | convolution fusion | flops 1074003968 | bytes 6291456 | tf_op jit(solution)/shard_map/dot_general | solution.py:113
  184.2 24.1 %all-to-all-done.8 = bf16[32,64,256]{2,1,0:T(8,128)(2,1)S(1)} async-done(((bf16[32,64,256]{2,1,0:T(8,128)(2,1)}), bf16[32,64,256]{2,1,0:T(8,128)(2,1)S(1)}, u32[]{:S(2)}, u32[]{:S(2)}) %all-to-all-start.8) | async-done | bytes 1048608 | tf_op jit(solution)/shard_map/all_to_all | solution.py:53
  209.4 4.0 %all-to-all-start.5 = ((f32[8,128,256]{2,1,0:T(8,128)}), f32[8,128,256]{2,1,0:T(8,128)S(1)}, u32[]{:S(2)}, u32[]{:S(2)}) async-start(f32[8,128,256]{2,1,0:T(8,128)} %bitcast.128), calls=%async_computation.5 | async-start | bytes 2097152 | tf_op jit(solution)/shard_map/all_to_all | solution.py:38
  214.7 12.6 %all-to-all-done.5 = f32[8,128,256]{2,1,0:T(8,128)S(1)} async-done(((f32[8,128,256]{2,1,0:T(8,128)}), f32[8,128,256]{2,1,0:T(8,128)S(1)}, u32[]{:S(2)}, u32[]{:S(2)}) %all-to-all-start.5) | async-done | bytes 1048608 | tf_op jit(solution)/shard_map/all_to_all | solution.py:38
  228.0 4.1 %all-to-all-start.9 = ((bf16[8,64,256]{2,1,0:T(8,128)(2,1)}), bf16[8,64,256]{2,1,0:T(8,128)(2,1)S(1)}, u32[]{:S(2)}, u32[]{:S(2)}) async-start(bf16[8,64,256]{2,1,0:T(8,128)(2,1)} %broadcast_in_dim.48), calls=%async_computation.9 | async-start | bytes 524288 | tf_op jit(solution)/shard_map/all_to_all | solution.py:44
  232.3 6.1 %all-to-all-done.9 = bf16[8,64,256]{2,1,0:T(8,128)(2,1)S(1)} async-done(((bf16[8,64,256]{2,1,0:T(8,128)(2,1)}), bf16[8,64,256]{2,1,0:T(8,128)(2,1)S(1)}, u32[]{:S(2)}, u32[]{:S(2)}) %all-to-all-start.9) | async-done | bytes 262176 | tf_op jit(solution)/shard_map/all_to_all | solution.py:44
  239.2 3.5 all-to-all-start.6
  245.5 4.6 %all-to-all-done.6 = bf16[8,128,256]{2,1,0:T(8,128)(2,1)S(1)} async-done(((bf16[8,128,256]{2,1,0:T(8,128)(2,1)}), bf16[8,128,256]{2,1,0:T(8,128)(2,1)S(1)}, u32[]{:S(2)}, u32[]{:S(2)}) %all-to-all-start.6) | async-done | bytes 524320 | tf_op jit(solution)/shard_map/all_to_all | solution.py:44
  250.1 9.3 %all-to-all-start.10 = ((bf16[256,1,8,128]{3,2,1,0:T(8,128)(2,1)}), bf16[256,1,8,128]{3,2,1,0:T(8,128)(2,1)S(1)}, u32[]{:S(2)}, u32[]{:S(2)}) async-start(bf16[256,1,8,128]{3,2,1,0:T(8,128)(2,1)} %copy.43), calls=%async_computation.10 | async-start | bytes 1048576 | tf_op jit(solution)/shard_map/all_to_all | solution.py:138
  261.8 15.8 %all-to-all-done.10 = bf16[256,1,8,128]{3,2,1,0:T(8,128)(2,1)S(1)} async-done(((bf16[256,1,8,128]{3,2,1,0:T(8,128)(2,1)}), bf16[256,1,8,128]{3,2,1,0:T(8,128)(2,1)S(1)}, u32[]{:S(2)}, u32[]{:S(2)}) %all-to-all-start.10) | async-done | bytes 524320 | tf_op jit(solution)/shard_map/all_to_all | solution.py:138
  278.4 4.7 %all-to-all-start.7 = ((bf16[256,2,8,128]{3,2,1,0:T(8,128)(2,1)}), bf16[256,2,8,128]{3,2,1,0:T(8,128)(2,1)S(1)}, u32[]{:S(2)}, u32[]{:S(2)}) async-start(bf16[256,2,8,128]{3,2,1,0:T(8,128)(2,1)} %copy.40), calls=%async_computation.7 | async-start | bytes 2097152 | tf_op jit(solution)/shard_map/all_to_all | solution.py:135
  285.6 18.3 %scatter_fusion.1 = f32[8,98,128]{2,0,1:T(8,128)S(1)} fusion(f32[8,98,128]{2,0,1:T(8,128)S(1)} %broadcast_in_dim.47, s32[256]{0:T(256)S(1)} %bitcast.135, f32[256,8,128]{2,1,0:T(8,128)} %bitcast.117), kind=kCustom, calls=%fused_computation.3 | custom fusion | flops 262144 | bytes 3146752 | tf_op jit(solution)/shard_map/scatter-add | solution.py:67
  303.9 8.1 %all-to-all-done.7 = bf16[256,2,8,128]{3,2,1,0:T(8,128)(2,1)S(1)} async-done(((bf16[256,2,8,128]{3,2,1,0:T(8,128)(2,1)}), bf16[256,2,8,128]{3,2,1,0:T(8,128)(2,1)S(1)}, u32[]{:S(2)}, u32[]{:S(2)}) %all-to-all-start.7) | async-done | bytes 1048608 | tf_op jit(solution)/shard_map/all_to_all | solution.py:135
  312.3 2.2 copy.41
  314.6 36.2 %scatter_fusion = f32[8,196,128]{2,0,1:T(8,128)S(1)} fusion(f32[8,196,128]{2,0,1:T(8,128)S(1)} %broadcast_in_dim.40, s32[512]{0:T(512)S(1)} %bitcast.133, f32[512,8,128]{2,1,0:T(8,128)} %bitcast.113), kind=kCustom, calls=%fused_computation.2 | custom fusion | flops 524288 | bytes 6293504 | tf_op jit(solution)/shard_map/scatter-add | solution.py:67
  (61 shorter events, 30.5 us)
Async XLA Ops:
  7.2 91.5 %copy-start = (bf16[2,1,8,512,128]{4,3,2,1,0:T(8,128)(2,1)S(1)}, bf16[2,1,8,512,128]{4,3,2,1,0:T(8,128)(2,1)}, u32[]{:S(2)}) copy-start(bf16[2,1,8,512,128]{4,3,2,1,0:T(8,128)(2,1)} %param.8) | copy-start | bytes 6291460
  7.2 38.1 %copy-start.5 = (bf16[8,25088]{1,0:T(8,128)(2,1)S(1)}, bf16[8,25088]{1,0:T(8,128)(2,1)}, u32[]{:S(2)}) copy-start(bf16[8,25088]{1,0:T(8,128)(2,1)} %param.12) | copy-start | bytes 1204228
  30.8 0.6 copy-start.7
  34.2 26.4 %all-to-all-start.3 = ((bf16[8,32,8,128]{3,2,0,1:T(8,128)(2,1)}), bf16[8,32,8,128]{3,2,0,1:T(8,128)(2,1)}, u32[]{:S(2)}, u32[]{:S(2)}) async-start(bf16[8,32,8,128]{3,2,0,1:T(8,128)(2,1)} %copy.36), calls=%async_computation.3 | async-start | bytes 1048576 | tf_op jit(solution)/shard_map/all_to_all | solution.py:81
  60.7 33.8 %all-to-all-start = ((bf16[8,64,8,128]{3,2,0,1:T(8,128)(2,1)}), bf16[8,64,8,128]{3,2,0,1:T(8,128)(2,1)S(1)}, u32[]{:S(2)}, u32[]{:S(2)}) async-start(bf16[8,64,8,128]{3,2,0,1:T(8,128)(2,1)} %copy_select_fusion), calls=%async_computation | async-start | bytes 2097152 | tf_op jit(solution)/shard_map/all_to_all | solution.py:80
  94.5 12.9 %all-to-all-start.4 = ((f32[8,64,256]{2,1,0:T(8,128)}), f32[8,64,256]{2,1,0:T(8,128)}, u32[]{:S(2)}, u32[]{:S(2)}) async-start(f32[8,64,256]{2,1,0:T(8,128)} %convolution_bitcast_fusion.1), calls=%async_computation.4 | async-start | bytes 1048576 | tf_op jit(solution)/shard_map/all_to_all | solution.py:38
  100.4 28.4 %copy-start.8 = (s32[2,32]{1,0:T(2,128)S(1)}, s32[2,32]{1,0:T(2,128)}, u32[]{:S(2)}) copy-start(s32[2,32]{1,0:T(2,128)} %param.14) | copy-start | bytes 772
  107.4 17.0 %all-to-all-start.1 = ((f32[8,128,256]{2,1,0:T(8,128)}), f32[8,128,256]{2,1,0:T(8,128)S(1)}, u32[]{:S(2)}, u32[]{:S(2)}) async-start(f32[8,128,256]{2,1,0:T(8,128)} %bitcast.20), calls=%async_computation.1 | async-start | bytes 2097152 | tf_op jit(solution)/shard_map/all_to_all | solution.py:38
  111.0 56.1 %all-gather.3.cloned.1.call-start = ((), (), s32[]{:S(2)}) async-start(), calls=%async_computation.11 | async-start | bytes 1081344 | tf_op jit(solution)/shard_map/all_gather | solution.py:92
  125.3 41.8 %all-to-all-start.2 = ((bf16[8,128,256]{2,1,0:T(8,128)(2,1)}), bf16[8,128,256]{2,1,0:T(8,128)(2,1)S(1)}, u32[]{:S(2)}, u32[]{:S(2)}) async-start(bf16[8,128,256]{2,1,0:T(8,128)(2,1)} %broadcast_in_dim.43), calls=%async_computation.2 | async-start | bytes 1048576 | tf_op jit(solution)/shard_map/all_to_all | solution.py:44
  171.0 2.4 copy-start.3
  173.5 34.9 %all-to-all-start.8 = ((bf16[32,64,256]{2,1,0:T(8,128)(2,1)}), bf16[32,64,256]{2,1,0:T(8,128)(2,1)S(1)}, u32[]{:S(2)}, u32[]{:S(2)}) async-start(bf16[32,64,256]{2,1,0:T(8,128)(2,1)} %bitcast.129), calls=%async_computation.8 | async-start | bytes 2097152 | tf_op jit(solution)/shard_map/all_to_all | solution.py:53
  208.4 1.0 copy-start.4
  209.4 18.0 %all-to-all-start.5 = ((f32[8,128,256]{2,1,0:T(8,128)}), f32[8,128,256]{2,1,0:T(8,128)S(1)}, u32[]{:S(2)}, u32[]{:S(2)}) async-start(f32[8,128,256]{2,1,0:T(8,128)} %bitcast.128), calls=%async_computation.5 | async-start | bytes 2097152 | tf_op jit(solution)/shard_map/all_to_all | solution.py:38
  228.0 10.3 %all-to-all-start.9 = ((bf16[8,64,256]{2,1,0:T(8,128)(2,1)}), bf16[8,64,256]{2,1,0:T(8,128)(2,1)S(1)}, u32[]{:S(2)}, u32[]{:S(2)}) async-start(bf16[8,64,256]{2,1,0:T(8,128)(2,1)} %broadcast_in_dim.48), calls=%async_computation.9 | async-start | bytes 524288 | tf_op jit(solution)/shard_map/all_to_all | solution.py:44
  239.2 11.0 %all-to-all-start.6 = ((bf16[8,128,256]{2,1,0:T(8,128)(2,1)}), bf16[8,128,256]{2,1,0:T(8,128)(2,1)S(1)}, u32[]{:S(2)}, u32[]{:S(2)}) async-start(bf16[8,128,256]{2,1,0:T(8,128)(2,1)} %broadcast_in_dim.46), calls=%async_computation.6 | async-start | bytes 1048576 | tf_op jit(solution)/shard_map/all_to_all | solution.py:44
  250.1 27.5 %all-to-all-start.10 = ((bf16[256,1,8,128]{3,2,1,0:T(8,128)(2,1)}), bf16[256,1,8,128]{3,2,1,0:T(8,128)(2,1)S(1)}, u32[]{:S(2)}, u32[]{:S(2)}) async-start(bf16[256,1,8,128]{3,2,1,0:T(8,128)(2,1)} %copy.43), calls=%async_computation.10 | async-start | bytes 1048576 | tf_op jit(solution)/shard_map/all_to_all | solution.py:138
  277.6 0.8 copy-start.6
  278.4 33.6 %all-to-all-start.7 = ((bf16[256,2,8,128]{3,2,1,0:T(8,128)(2,1)}), bf16[256,2,8,128]{3,2,1,0:T(8,128)(2,1)S(1)}, u32[]{:S(2)}, u32[]{:S(2)}) async-start(bf16[256,2,8,128]{3,2,1,0:T(8,128)(2,1)} %copy.40), calls=%async_computation.7 | async-start | bytes 2097152 | tf_op jit(solution)/shard_map/all_to_all | solution.py:135
  303.9 46.8 %copy-start.2 = (f32[8,98,128]{2,0,1:T(8,128)}, f32[8,98,128]{2,0,1:T(8,128)S(1)}, u32[]{:S(2)}) copy-start(f32[8,98,128]{2,0,1:T(8,128)S(1)} %scatter_fusion.1) | copy-start | bytes 1204228
  350.7 0.9 copy-start.1
Sparse Core Ops, SparseCore 0:
  114.9 52.1 all-gather.2
where the time goes:
time: 362 us; the launch traced here: 358 us
  waiting for transfers between devices  163 us (45%)
  other arithmetic  64.1 us (18%)
  starting transfers between devices  56.1 us (15%)
  local copies, waits for them, and re-layouts  23.2 us (6%)
  blocking collectives  18.8 us (5%)
  matrix products  18.1 us (5%)
  between operations  15 us (4%)
    scatter-add x2, other arithmetic, accumulate(): totals.at[:, indices.reshape(-1)].add(returned.reshape(rank_part, -1, FBW))  54.5 us
    all_gather x1, waiting for transfers between devices, on_device(): item_all = lax.all_gather(item_share, 'rows', axis=0, tiled=True)  38.1 us
    all_to_all x3, waiting for transfers between devices, sent_and_summed(): tiles = lax.all_to_all(split_up(shard, dim, size), axis, 0, 0, tiled=True)  28.6 us
    all_to_all x1, waiting for transfers between devices, on_device(): lax.all_to_all(user_ask, 'rows', split_axis=1, concat_axis=0, tiled=True)  26.3 us
    all_to_all x1, waiting for transfers between devices, sum_at_owner(): lax.all_to_all(tiles, axis, split_axis=0, concat_axis=0, tiled=True)  24.1 us
    unnamed x1, blocking collectives  18.8 us
    all_to_all x1, waiting for transfers between devices, on_device(): lax.all_to_all(item_grad_blocks.astype(jnp.bfloat16), 'rows', split_axis=...  15.8 us
    all_to_all x3, starting transfers between devices, sent_and_summed(): tiles = lax.all_to_all(split_up(shard, dim, size), axis, 0, 0, tiled=True)  11.8 us
  transfers between devices with their start and end apart: 12, of which 11 were waited for; matrix products, arithmetic and copies ran while one was open for 14% of the time, Pallas kernels for 0%

commit v1 on v0

v1 whole, which is shorter than its diff:
```python
import math

import jax
import jax.numpy as jnp
from jax import lax
from jax.experimental import pallas as pl
from jax.experimental.pallas import tpu as pltpu
from jax.sharding import PartitionSpec as P

TILE = 512
FBW = 128
RANK = 256
ROWS = 32
FEAT = 8
NX = 4
NZ = 4
K = 8
SH = TILE // FEAT
RP = RANK // ROWS
MESH = pl.DeviceIdType.MESH

IDX, A0, B0, C0, IZ, IX, IC, D0, DG0, EC, EX, EZ, FG, G0, NCH = (
    0, 1, 4, 7, 9, 10, 11, 12, 14, 16, 17, 18, 19, 20, 23)

NT = (((1,), (1,)), ((), ()))
NN = (((1,), (0,)), ((), ()))


def dot(a, b, dims):
    return lax.dot_general(a, b, dims, preferred_element_type=jnp.float32)


def kernel(idx_in, mask, wu_h, wi_h, x_h, y_h, rat_h, grecv, idx_all,
           wu, wi, wu3, wi3, xv, rat, idx_s, asend, arecv, wcat, part, rsr, share, upb,
           item_all, gacc, tacc, gpart, gpr, gshare, gfull, ebuf, ecr, es, exr,
           ez, ezr, gsend, upt, lsem, ssem, rsem):
    row = lax.axis_index("rows")
    feat = lax.axis_index("feat")
    mx = row // (2 * NZ)
    mz = lax.rem(row // 2, NZ)
    mc = lax.rem(row, 2)
    rank_scale = 1.0 / math.sqrt(RANK)
    grad_scale = 1.0 / (TILE * math.sqrt(RANK))

    def row_of(dx, dz, dc):
        return (lax.rem(mx + dx, NX) * (2 * NZ) + lax.rem(mz + dz, NZ) * 2
                + lax.rem(mc + dc, 2))

    def row_peer(j):
        return row_of(lax.rem(j // NZ, NX), lax.rem(j, NZ), j // (NX * NZ))

    def feat_peer(j):
        return lax.rem(feat + j, FEAT)

    def send(src, dst, ch, rows=None, f=None):
        pltpu.make_async_remote_copy(
            src_ref=src, dst_ref=dst, send_sem=ssem.at[ch], recv_sem=rsem.at[ch],
            device_id={"rows": row if rows is None else rows, "feat": feat if f is None else f},
            device_id_type=MESH).start()

    def bulk(ref, ch):
        return pltpu.make_async_remote_copy(
            src_ref=ref, dst_ref=ref, send_sem=ssem.at[ch], recv_sem=rsem.at[ch],
            device_id={"rows": row_of(0, 0, 1), "feat": feat}, device_id_type=MESH)

    loads = [
        pltpu.make_async_copy(wi_h, wi, lsem.at[0]),
        pltpu.make_async_copy(wu_h, wu, lsem.at[1]),
        pltpu.make_async_copy(y_h, xv.at[pl.ds(0, K)], lsem.at[2]),
        pltpu.make_async_copy(x_h, xv.at[pl.ds(K, 2 * K)], lsem.at[3]),
        pltpu.make_async_copy(rat_h, rat, lsem.at[4]),
    ]
    for c in loads:
        c.start()
    for c, table, blocks in ((loads[0], wi, wi3), (loads[1], wu, wu3)):
        c.wait()
        for i in range(blocks.shape[0]):
            blocks[i] = table[:, i * FBW:(i + 1) * FBW]

    barrier = pltpu.get_barrier_semaphore()

    @pl.loop(1, ROWS)
    def _(j):
        pl.semaphore_signal(barrier, inc=1, device_id={"rows": row_peer(j), "feat": feat},
                            device_id_type=MESH)

    @pl.loop(1, FEAT)
    def _(j):
        pl.semaphore_signal(barrier, inc=1, device_id={"rows": row, "feat": feat_peer(j)},
                            device_id_type=MESH)
    pl.semaphore_wait(barrier, ROWS - 1 + FEAT - 1)

    @pl.loop(1, ROWS)
    def _(j):
        send(idx_in.at[0], idx_all.at[row], IDX, rows=row_peer(ROWS - j))
    idx_all[row] = idx_in[0]
    bulk(idx_all.at[pl.ds(0, ROWS - 1)], IDX).wait_recv()
    to_smem = pltpu.make_async_copy(idx_all, idx_s, lsem.at[5])
    to_smem.start()
    to_smem.wait()

    def pick(table, dst, d, unit):
        for k in range(K):
            dst[k] = table[idx_s[d, 0, unit * K + k]]

    for unit in range(3):
        table = wi3 if unit == 0 else wu3

        @pl.loop(1, ROWS)
        def _(j):
            d = row_peer(ROWS - j)
            pick(table, asend.at[unit, d], d, unit)
            send(asend.at[unit, d], arecv.at[unit, row], A0 + unit, rows=d)
        pick(table, arecv.at[unit, row], row, unit)

    for c in loads[2:]:
        c.wait()

    def project(unit):
        bulk(arecv.at[unit, pl.ds(0, ROWS - 1)], A0 + unit).wait_recv()
        for k in range(K):
            w = arecv[unit, :, k].astype(jnp.float32).reshape(RANK, FBW)
            wcat[:, k * FBW:(k + 1) * FBW] = w.astype(jnp.bfloat16)
        half = FEAT // 2
        for h in range(2):
            xt = jnp.concatenate(
                [xv[unit * K + k, h * half * SH:(h + 1) * half * SH] for k in range(K)], axis=1)
            p = dot(xt, wcat[...], NT)
            part[unit, h * half:(h + 1) * half] = p.astype(jnp.bfloat16).reshape(half, SH, RANK)

    def scatter(src, dst, ch):
        @pl.loop(1, FEAT)
        def _(j):
            f = feat_peer(FEAT - j)
            send(src.at[f], dst.at[feat], ch, f=f)
        dst[feat] = src[feat]

    def summed(dst, ch):
        bulk(dst.at[pl.ds(0, FEAT - 1)], ch).wait_recv()
        total = dst[0].astype(jnp.float32)
        for f in range(1, FEAT):
            total = total + dst[f].astype(jnp.float32)
        return total.astype(jnp.bfloat16)

    def gather(src, dst, ch):
        @pl.loop(1, FEAT)
        def _(j):
            send(src, dst.at[feat], ch, f=feat_peer(FEAT - j))
        dst[feat] = src[...]

    def wait_gather(dst, ch):
        bulk(dst.at[pl.ds(0, FEAT - 1)], ch).wait_recv()

    def residual(b):
        up = upb[b].reshape(TILE, RANK)
        upt[...] = up.T
        gacc[...] = jnp.zeros_like(gacc)

        @pl.loop(0, 2 * NX)
        def _(q):
            x = q // 2
            z = lax.rem(q, 2) * 2
            it = jnp.concatenate(
                [item_all[c, x, z + dz] for dz in range(2) for c in range(2)], axis=0)
            cols = pl.ds(pl.multiple_of(q * RANK, RANK), RANK)
            pred = dot(upb[b].reshape(TILE, RANK), it, NT) * rank_scale
            r = mask[b:b + 1, cols] * (
                pred - rat[b * TILE:(b + 1) * TILE, cols].astype(jnp.float32))
            r = r.astype(jnp.bfloat16)
            gacc[...] += dot(r, it, NN)
            t = dot(upt[...], r, NN)
            if b == 0:
                tacc[:, cols] = t
            else:
                tacc[:, cols] += t
        gpart[b] = (gacc[...] * grad_scale).astype(jnp.bfloat16).reshape(FEAT, SH, RANK)

    def block_grads(unit):
        gt = gfull[unit].reshape(TILE, RANK).T
        for k in range(0, K, 2):
            two = jnp.concatenate([xv[unit * K + k], xv[unit * K + k + 1]], axis=1)
            o = dot(gt, two, NN)
            for i in range(2):
                s = o[:, i * FBW:(i + 1) * FBW].reshape(ROWS, RP, FBW)
                gsend[unit, :, k + i] = s.astype(jnp.bfloat16)

        @pl.loop(1, ROWS)
        def _(j):
            d = row_peer(ROWS - j)
            send(gsend.at[unit, d], grecv.at[unit, row], G0 + unit, rows=d)
        grecv[unit, row] = gsend[unit, row]

    project(0)
    scatter(part.at[0], rsr.at[0], B0)
    share[0] = summed(rsr.at[0], B0)
    item_all[mc, mx, mz] = share[0]
    for dz in (2, 1, 3):
        send(share.at[0], item_all.at[mc, mx, mz], IZ, rows=row_of(0, dz, 0))
    bulk(item_all.at[0, 0, pl.ds(0, NZ - 1)], IZ).wait_recv()
    for dx in (2, 1, 3):
        send(item_all.at[mc, mx], item_all.at[mc, mx], IX, rows=row_of(dx, 0, 0))
    bulk(item_all.at[0, pl.ds(0, NX - 1)], IX).wait_recv()
    send(item_all.at[mc], item_all.at[mc], IC, rows=row_of(0, 0, 1))

    project(1)
    scatter(part.at[1], rsr.at[1], B0 + 1)
    share[1] = summed(rsr.at[1], B0 + 1)
    gather(share.at[1], upb.at[0], C0)
    bulk(item_all.at[0], IC).wait_recv()
    wait_gather(upb.at[0], C0)
    residual(0)
    scatter(gpart.at[0], gpr.at[0], D0)

    project(2)
    scatter(part.at[2], rsr.at[2], B0 + 2)
    gshare[1] = summed(gpr.at[0], D0)
    gather(gshare.at[1], gfull.at[1], DG0)
    share[2] = summed(rsr.at[2], B0 + 2)
    gather(share.at[2], upb.at[1], C0 + 1)
    wait_gather(gfull.at[1], DG0)
    block_grads(1)
    wait_gather(upb.at[1], C0 + 1)
    residual(1)
    scatter(gpart.at[1], gpr.at[1], D0 + 1)

    @pl.loop(0, 2 * NX)
    def _(q):
        x = q // 2
        z = lax.rem(q, 2) * 2
        cols = pl.ds(pl.multiple_of(q * RANK, RANK), RANK)
        t = (tacc[:, cols] * grad_scale).T.astype(jnp.bfloat16)
        for dz in range(2):
            for c in range(2):
                i = dz * 2 + c
                ebuf[c, x, z + dz] = t[i * SH:(i + 1) * SH]
    send(ebuf.at[1 - mc], ecr, EC, rows=row_of(0, 0, 1))
    gshare[2] = summed(gpr.at[1], D0 + 1)
    gather(gshare.at[2], gfull.at[2], DG0 + 1)
    bulk(ecr, EC).wait_recv()

    @pl.loop(0, NX)
    def _(x):
        es[x] = (ebuf[mc, x].astype(jnp.float32)
                 + ecr[x].astype(jnp.float32)).astype(jnp.bfloat16)
    for dx in (2, 1, 3):
        x = lax.rem(mx + dx, NX)
        send(es.at[x], exr.at[mx], EX, rows=row_of(dx, 0, 0))
    exr[mx] = es[mx]
    wait_gather(gfull.at[2], DG0 + 1)
    block_grads(2)
    bulk(exr.at[pl.ds(0, NX - 1)], EX).wait_recv()
    for z in range(NZ):
        total = exr[0, z].astype(jnp.float32)
        for x in range(1, NX):
            total = total + exr[x, z].astype(jnp.float32)
        ez[z] = total.astype(jnp.bfloat16)
    for dz in (2, 1, 3):
        z = lax.rem(mz + dz, NZ)
        send(ez.at[z], ezr.at[mz], EZ, rows=row_of(0, dz, 0))
    ezr[mz] = ez[mz]
    bulk(ezr.at[pl.ds(0, NZ - 1)], EZ).wait_recv()
    total = ezr[0].astype(jnp.float32)
    for z in range(1, NZ):
        total = total + ezr[z].astype(jnp.float32)
    gshare[0] = total.astype(jnp.bfloat16)
    gather(gshare.at[0], gfull.at[0], FG)
    wait_gather(gfull.at[0], FG)
    block_grads(0)

    for u in (1, 2, 0):
        bulk(grecv.at[u, pl.ds(0, ROWS - 1)], G0 + u).wait_recv()

    bulk(idx_all.at[pl.ds(0, ROWS - 1)], IDX).wait_send()
    for u in range(3):
        bulk(asend.at[u, pl.ds(0, ROWS - 1)], A0 + u).wait_send()
        bulk(rsr.at[u, pl.ds(0, FEAT - 1)], B0 + u).wait_send()
        bulk(gsend.at[u, pl.ds(0, ROWS - 1)], G0 + u).wait_send()
    for b in range(2):
        bulk(upb.at[b, pl.ds(0, FEAT - 1)], C0 + b).wait_send()
        bulk(gpr.at[b, pl.ds(0, FEAT - 1)], D0 + b).wait_send()
        bulk(gfull.at[b, pl.ds(0, FEAT - 1)], DG0 + b).wait_send()
    bulk(item_all.at[0, 0, pl.ds(0, NZ - 1)], IZ).wait_send()
    bulk(item_all.at[0, pl.ds(0, NX - 1)], IX).wait_send()
    bulk(item_all.at[0], IC).wait_send()
    bulk(ecr, EC).wait_send()
    bulk(exr.at[pl.ds(0, NX - 1)], EX).wait_send()
    bulk(ezr.at[pl.ds(0, NZ - 1)], EZ).wait_send()
    bulk(gfull.at[0, pl.ds(0, FEAT - 1)], FG).wait_send()


def accumulate(returned, ids, blocks):
    onehot = (ids.reshape(-1)[:, None] == jnp.arange(blocks, dtype=jnp.int32)[None, :])
    totals = jnp.einsum("prc,pn->rnc", returned.reshape(-1, RP, FBW),
                        onehot.astype(jnp.bfloat16), preferred_element_type=jnp.float32)
    return totals.reshape(RP, blocks * FBW)


def on_device(x_vals, x_blocks, y_vals, y_blocks, user_weights, item_weights, observed, ratings):
    ids = jnp.concatenate([y_blocks.reshape(-1), x_blocks.reshape(-1)])
    ids = jnp.pad(ids, (0, FBW - 3 * K)).reshape(1, 1, FBW)
    mask = jnp.repeat(observed.astype(jnp.float32), SH, axis=1)
    bf, f32 = jnp.bfloat16, jnp.float32
    V = pltpu.VMEM
    grecv, idx_all = pl.pallas_call(
        kernel,
        out_shape=(jax.ShapeDtypeStruct((3, ROWS, K, RP, FBW), bf),
                   jax.ShapeDtypeStruct((ROWS, 1, FBW), jnp.int32)),
        in_specs=[pl.BlockSpec(memory_space=pltpu.VMEM)] * 2
        + [pl.BlockSpec(memory_space=pl.ANY)] * 5,
        out_specs=[pl.BlockSpec(memory_space=pltpu.VMEM)] * 2,
        scratch_shapes=[
            V(user_weights.shape, bf), V(item_weights.shape, bf),
            V((user_weights.shape[1] // FBW, RP, FBW), bf),
            V((item_weights.shape[1] // FBW, RP, FBW), bf), V((3 * K, TILE, FBW), bf),
            V((2 * TILE, ROWS * SH), bf), pltpu.SMEM((ROWS, 1, FBW), jnp.int32),
            V((3, ROWS, K, RP, FBW), bf), V((3, ROWS, K, RP, FBW), bf), V((RANK, K * FBW), bf),
            V((3, FEAT, SH, RANK), bf), V((3, FEAT, SH, RANK), bf), V((3, SH, RANK), bf),
            V((2, FEAT, SH, RANK), bf), V((2, NX, NZ, SH, RANK), bf), V((TILE, RANK), f32),
            V((RANK, ROWS * SH), f32), V((2, FEAT, SH, RANK), bf), V((2, FEAT, SH, RANK), bf),
            V((3, SH, RANK), bf), V((3, FEAT, SH, RANK), bf), V((2, NX, NZ, SH, RANK), bf),
            V((NX, NZ, SH, RANK), bf), V((NX, NZ, SH, RANK), bf), V((NX, NZ, SH, RANK), bf),
            V((NZ, SH, RANK), bf), V((NZ, SH, RANK), bf), V((3, ROWS, K, RP, FBW), bf),
            V((RANK, TILE), bf), pltpu.SemaphoreType.DMA((6,)),
            pltpu.SemaphoreType.DMA((NCH,)), pltpu.SemaphoreType.DMA((NCH,)),
        ],
        compiler_params=pltpu.CompilerParams(
            collective_id=0, has_side_effects=True),
        name="step",
    )(ids, mask, user_weights, item_weights, x_vals.reshape(2 * K, TILE, FBW),
      y_vals.reshape(K, TILE, FBW), ratings.reshape(2 * TILE, ROWS * SH))
    ids_all = idx_all[:, 0, :3 * K].reshape(ROWS, 3, K).swapaxes(0, 1)
    return (accumulate(grecv[1:], ids_all[1:], user_weights.shape[1] // FBW),
            accumulate(grecv[0], ids_all[0], item_weights.shape[1] // FBW))


def solution(mesh):
    return jax.shard_map(
        on_device,
        mesh=mesh,
        in_specs=(
            P("rows", "feat", None, None, None),
            P("rows", "feat", None),
            P("rows", "feat", None, None, None),
            P("rows", "feat", None),
            P("rows", "feat"),
            P("rows", "feat"),
            P("rows", None),
            P("rows", "feat", None),
        ),
        out_specs=(P("rows", "feat"), P("rows", "feat")),
        check_vma=False,
    )
```

time: 362 us -> 164 us (0.45)
  waiting for transfers between devices: 163 us -> 0 us
  Pallas kernels: 0 us -> 153 us
  other arithmetic: 64.1 us -> 2.75 us
  starting transfers between devices: 56.1 us -> 0 us
  blocking collectives: 18.8 us -> 0 us
  matrix products: 18.1 us -> 0.63 us
  local copies, waits for them, and re-layouts: 23.2 us -> 6.13 us
  between operations: 15 us -> 0.68 us
    pallas_call x0 -> x1, Pallas kernels: none -> 153 us  [on_device(): pl.pallas_call(kernel, out_shape=(jax.ShapeDtypeStruct((3, ROWS, K, RP, F...]
    all_to_all x11 -> x0, waiting for transfers between devices: 125 us -> none  [the longest x3 28.6 us: sent_and_summed(): tiles = lax.all_to_all(split_up(shard, dim, size), axis, 0, 0, tiled=True)]
    all_to_all x11 -> x0, starting transfers between devices: 56 us -> none  [the longest x3 11.8 us: sent_and_summed(): tiles = lax.all_to_all(split_up(shard, dim, size), axis, 0, 0, tiled=True)]
    scatter-add x2 -> x0, other arithmetic: 54.5 us -> none  [accumulate(): totals.at[:, indices.reshape(-1)].add(returned.reshape(rank_part, -1, FBW))]
    all_gather x1 -> x0, waiting for transfers between devices: 38.1 us -> none  [on_device(): item_all = lax.all_gather(item_share, 'rows', axis=0, tiled=True)]
    unnamed x1 -> x0, blocking collectives: 18.8 us -> none
    dot_general x8 -> x2, matrix products: 18.1 us -> 0.63 us  [accumulate(): jnp.einsum('prc,pn->rnc', returned.reshape(-1, RP, FBW), onehot.astype(jn...]
    convert_element_type x4 -> x0, local copies, waits for them, and re-layouts: 6.26 us -> none  [the longest x2 3.43 us: on_device(): back_user, back_item = (lax.all_to_all(user_grad_blocks.astype(jnp.bfloat...]
  transfers between devices with their start and end apart: 12 -> 0, of which waited for: 11 -> 0; matrix products, arithmetic and copies ran while one was open for 14% -> 0% of each run, Pallas kernels for 0% -> 0%
where the time goes in v1:
time: 164 us; the launch traced here: 163 us
  Pallas kernels  153 us (93%)
  local copies, waits for them, and re-layouts  6.13 us (4%)
  other arithmetic  2.75 us (2%)
    pallas_call x1, Pallas kernels, on_device(): pl.pallas_call(kernel, out_shape=(jax.ShapeDtypeStruct((3, ROWS, K, RP, F...  153 us

profile of v1, /device:TPU:1, one launch (start us, length us, event | category | flops | bytes accessed | tf_op | source)
XLA Modules:
  0.0 162.8 jit_solution(1491830535898336682)
XLA Ops:
  0.6 0.7 convert_element_type.2
  1.3 0.1 broadcast_in_dim.2
  1.4 0.7 reshape.39.mask
  2.1 0.5 broadcast.5
  2.6 1.3 reduce.3
  3.9 0.1 reshape.37
  4.0 0.7 pad_add_fusion
  4.7 0.5 pad_bitcast_fusion.idx_in
  5.3 152.6 %step.1 = (bf16[3,32,8,8,128]{4,3,2,1,0:T(8,128)(2,1)}, s32[32,1,128]{2,1,0:T(1,128)}) custom-call(s32[1,1,128]{2,1,0:T(1,128)} %pad_bitcast_fusion.idx_in, f32[2,2048]{1,0:T(2,128)} %reshape.39.mask, bf16[8,25088]{1,0:T(8,128)(2,1)} %wu_h.1, bf16[8,12544]{1,0:T(8,128)(2,1)} %wi_h.1, bf16[16,512,128]{2,1,0:T(8,128)(2,1)} %bitcast.32, ...), custom_call_target="tpu_custom_call" | custom-call | tf_op jit(solution)/shard_map/step/pallas_call | solution.py:304
  157.9 0.0 copy-start
  157.9 1.2 slice.19
  159.1 0.8 copy.12
  159.9 0.1 copy.15
  160.0 0.1 eq.34
  160.1 0.2 convolution_bitcast_fusion.1
  160.3 0.8 copy.26
  161.2 0.0 copy-done
  161.2 0.1 slice.17
  161.2 0.1 copy.13
  161.3 0.1 eq.30
  161.4 0.4 convolution_bitcast_fusion
  161.8 1.0 copy.25
  (2 shorter events, 0.0 us)
Async XLA Ops:
  157.9 3.2 %copy-start = (bf16[3,32,8,8,128]{4,3,2,1,0:T(8,128)(2,1)S(1)}, bf16[3,32,8,8,128]{4,3,2,1,0:T(8,128)(2,1)}, u32[]{:S(2)}) copy-start(bf16[3,32,8,8,128]{4,3,2,1,0:T(8,128)(2,1)} %get-tuple-element.5) | copy-start | bytes 4718596

commit v2 on v1

v2 whole, which is shorter than its diff:
```python
import math

import jax
import jax.numpy as jnp
from jax import lax
from jax.experimental import pallas as pl
from jax.experimental.pallas import tpu as pltpu
from jax.sharding import PartitionSpec as P

TILE = 512
FBW = 128
RANK = 256
ROWS = 32
FEAT = 8
NX = 4
NZ = 4
K = 8
SH = TILE // FEAT
NY = FEAT // 2
RP = RANK // ROWS
MESH = pl.DeviceIdType.MESH

IDX, A0, BY, BL, IZ, IX, IC, EC, EX, EZ, FL, FY, G0, UY, UL, UG, NCH = (
    0, 1, 4, 5, 6, 7, 8, 9, 10, 11, 12, 13, 14, 17, 21, 25, 29)

NT = (((1,), (1,)), ((), ()))
NN = (((1,), (0,)), ((), ()))


def dot(a, b, dims):
    return lax.dot_general(a, b, dims, preferred_element_type=jnp.float32)


def kernel(x_idx, y_idx, observed, wu_h, wi_h, x_h, y_h, rat_h, gru, gri, idx_all,
           wu, wi, wu3, wi3, xv, rat, mask, idx_loc, idx_s, asend, arecv, wcat, ipart,
           iyr, iys, ilr, ishare, apart, ayr, ays, alr, full, item_all, resid, tacc,
           ebuf, ecr, es, exr, ez, ezr, ifull, gsend, upt, lsem, ssem, rsem):
    row = lax.axis_index("rows")
    feat = lax.axis_index("feat")
    mx = row // (2 * NZ)
    mz = lax.rem(row // 2, NZ)
    mc = lax.rem(row, 2)
    my = feat // 2
    ml = lax.rem(feat, 2)
    bf, f32 = jnp.bfloat16, jnp.float32
    rank_scale = 1.0 / math.sqrt(RANK)
    grad_scale = 1.0 / (TILE * math.sqrt(RANK))

    def row_of(dx, dz, dc):
        return (lax.rem(mx + dx, NX) * (2 * NZ) + lax.rem(mz + dz, NZ) * 2
                + lax.rem(mc + dc, 2))

    def row_peer(j):
        return row_of(lax.rem(j // NZ, NX), lax.rem(j, NZ), j // (NX * NZ))

    def feat_of(dy, dl):
        return lax.rem(my + dy, NY) * 2 + lax.rem(ml + dl, 2)

    def copy(src, dst, ch, rows=None, f=None):
        return pltpu.make_async_remote_copy(
            src_ref=src, dst_ref=dst, send_sem=ssem.at[ch], recv_sem=rsem.at[ch],
            device_id={"rows": row if rows is None else rows, "feat": feat if f is None else f},
            device_id_type=MESH)

    unsent = []

    def send(src, dst, ch, rows=None, f=None):
        copy(src, dst, ch, rows, f).start()

    def arrived(ref, ch):
        c = copy(ref, ref, ch, rows=row_of(0, 0, 1))
        c.wait_recv()
        unsent.append(c)

    barrier = pltpu.get_barrier_semaphore()

    @pl.loop(1, ROWS)
    def _(j):
        pl.semaphore_signal(barrier, inc=1, device_id={"rows": row_peer(ROWS - j), "feat": feat},
                            device_id_type=MESH)
    feat_peers = [(0, 1)] + [(dy, 0) for dy in (2, 1, 3)]
    for dy, dl in feat_peers:
        pl.semaphore_signal(barrier, inc=1, device_id={"rows": row, "feat": feat_of(dy, dl)},
                            device_id_type=MESH)

    loads = [
        pltpu.make_async_copy(wi_h, wi, lsem.at[0]),
        pltpu.make_async_copy(wu_h, wu, lsem.at[1]),
        pltpu.make_async_copy(y_h, xv.at[pl.ds(0, K)], lsem.at[2]),
        pltpu.make_async_copy(x_h, xv.at[pl.ds(K, 2 * K)], lsem.at[3]),
        pltpu.make_async_copy(rat_h, rat, lsem.at[4]),
    ]
    for c in loads:
        c.start()
    idx_loc[...] = jnp.zeros_like(idx_loc)
    idx_loc[0:1, 0:K] = y_idx[...]
    idx_loc[1:3, 0:K] = x_idx[...]
    left = lax.broadcasted_iota(jnp.int32, (1, 2 * SH), 1) < SH
    for b in range(2):
        for p in range(ROWS // 2):
            pair = jnp.where(left, observed[b, 2 * p], observed[b, 2 * p + 1])
            mask[b:b + 1, p * 2 * SH:(p + 1) * 2 * SH] = pair.astype(f32)
    for c, table, blocks in ((loads[0], wi, wi3), (loads[1], wu, wu3)):
        c.wait()
        for i in range(blocks.shape[0]):
            blocks[i] = table[:, i * FBW:(i + 1) * FBW]
    pl.semaphore_wait(barrier, ROWS - 1 + len(feat_peers))

    @pl.loop(1, ROWS)
    def _(j):
        send(idx_loc, idx_all.at[row], IDX, rows=row_peer(ROWS - j))
    idx_all[row] = idx_loc[...]
    arrived(idx_all.at[pl.ds(0, ROWS - 1)], IDX)
    to_smem = pltpu.make_async_copy(idx_all, idx_s, lsem.at[5])
    to_smem.start()
    to_smem.wait()

    def pick(unit, dst, d):
        table = wi3 if unit == 0 else wu3
        for k in range(K):
            dst[k] = table[idx_s[d, unit, k]]

    def ask(unit, lo, hi, picks=True, sends=True):
        @pl.loop(lo, hi)
        def _(j):
            d = row_peer(ROWS - j)
            if picks:
                pick(unit, asend.at[unit, d], d)
            if sends:
                send(asend.at[unit, d], arecv.at[unit, row], A0 + unit, rows=d)

    def project(unit, dst):
        arrived(arecv.at[unit, pl.ds(0, ROWS - 1)], A0 + unit)
        for k in range(K):
            w = arecv[unit, :, k].astype(f32).reshape(RANK, FBW)
            wcat[:, k * FBW:(k + 1) * FBW] = w.astype(bf)
        half = TILE // 2
        for h in range(2):
            xt = jnp.concatenate(
                [xv[unit * K + k, h * half:(h + 1) * half] for k in range(K)], axis=1)
            p = dot(xt, wcat[...], NT)
            dst[h * 2:(h + 1) * 2] = p.astype(bf).reshape(2, 2, SH, RANK)

    def y_scatter(src, dst, ch):
        for dy in (2, 1, 3):
            y = lax.rem(my + dy, NY)
            send(src.at[y], dst.at[my], ch, f=feat_of(dy, 0))
        dst[my] = src[my]

    def y_sum(dst, out, ch):
        arrived(dst.at[pl.ds(0, NY - 1)], ch)
        for l in range(2):
            total = dst[0, l].astype(f32)
            for y in range(1, NY):
                total = total + dst[y, l].astype(f32)
            out[l] = total.astype(bf)

    def y_gather(dst, ch):
        for dy in (2, 1, 3):
            send(dst.at[my], dst.at[my], ch, f=feat_of(dy, 0))

    def y_full(dst, ch):
        arrived(dst.at[pl.ds(0, NY - 1)], ch)

    def s_send(i):
        y_scatter(apart.at[i], ayr.at[i], UY + i)

    def s_mid(i):
        y_sum(ayr.at[i], ays.at[i], UY + i)
        send(ays.at[i], alr.at[i], UL + i, f=feat_of(0, 1))

    def s_out(i):
        arrived(alr.at[i], UL + i)
        full[i, my] = (ays[i].astype(f32) + alr[i].astype(f32)).astype(bf)
        y_gather(full.at[i], UG + i)

    def s_wait(i):
        y_full(full.at[i], UG + i)

    def residual(b):
        upt[...] = full[b].reshape(TILE, RANK).T

        @pl.loop(0, NX)
        def _(x):
            it = item_all[x].reshape(2 * TILE // 2, RANK)
            cols = pl.ds(pl.multiple_of(x * TILE, TILE), TILE)
            pred = dot(full[b].reshape(TILE, RANK), it, NT) * rank_scale
            r = mask[b:b + 1, cols] * (pred - rat[b * TILE:(b + 1) * TILE, cols].astype(f32))
            r = r.astype(bf)
            resid[:, cols] = r
            t = dot(upt[...], r, NN)
            if b == 0:
                tacc[:, cols] = t
            else:
                tacc[:, cols] += t
        for h in range(2):
            g = dot(resid[h * RANK:(h + 1) * RANK, :], item_all[...].reshape(ROWS * SH, RANK), NN)
            apart[2 + b, h * 2:(h + 1) * 2] = (g * grad_scale).astype(bf).reshape(2, 2, SH, RANK)

    def block_grads(unit, src, out):
        gt = src[...].reshape(TILE, RANK).T
        for k in range(0, K, 2):
            two = jnp.concatenate([xv[unit * K + k], xv[unit * K + k + 1]], axis=1)
            o = dot(gt, two, NN)
            for i in range(2):
                s = o[:, i * FBW:(i + 1) * FBW].reshape(ROWS, RP, FBW)
                gsend[unit, :, k + i] = s.astype(bf)
        out[row] = gsend[unit, row]

    def give(unit, out, lo, hi):
        @pl.loop(lo, hi)
        def _(j):
            d = row_peer(ROWS - j)
            send(gsend.at[unit, d], out.at[row], G0 + unit, rows=d)

    ask(0, 1, ROWS)
    ask(1, 1, ROWS)
    for unit in range(3):
        pick(unit, arecv.at[unit, row], row)
    for c in loads[2:]:
        c.wait()
    project(0, ipart)
    y_scatter(ipart, iyr, BY)
    ask(2, 1, ROWS, sends=False)
    y_sum(iyr, iys, BY)
    send(iys.at[1 - ml], ilr, BL, f=feat_of(0, 1))
    ask(2, 1, HALF, picks=False)
    project(1, apart.at[0])
    s_send(0)
    arrived(ilr, BL)
    ishare[...] = (iys[ml].astype(f32) + ilr[...].astype(f32)).astype(bf)
    item_all[mx, mz, mc] = ishare[...]
    for dz in (2, 1, 3):
        send(ishare, item_all.at[mx, mz, mc], IZ, rows=row_of(0, dz, 0))
    ask(2, HALF, ROWS, picks=False)
    s_mid(0)
    arrived(item_all.at[0, pl.ds(0, NZ - 1), 0], IZ)
    for dx in (2, 1, 3):
        send(item_all.at[mx, :, mc], item_all.at[mx, :, mc], IX, rows=row_of(dx, 0, 0))
    s_out(0)
    arrived(item_all.at[pl.ds(0, NX - 1), :, 0], IX)
    send(item_all.at[:, :, mc], item_all.at[:, :, mc], IC, rows=row_of(0, 0, 1))
    project(2, apart.at[1])
    s_send(1)
    arrived(item_all.at[:, :, 0], IC)
    s_wait(0)
    residual(0)
    s_send(2)
    s_mid(1)
    s_out(1)
    s_mid(2)
    s_out(2)
    s_wait(1)
    residual(1)
    s_send(3)
    s_wait(2)
    block_grads(1, full.at[2], gru.at[0])
    give(1, gru.at[0], 1, HALF)

    for q in range(2 * NX):
        t = (tacc[:, q * RANK:(q + 1) * RANK] * grad_scale).T.astype(bf)
        for i in range(4):
            g = q * 4 + i
            ebuf[g // (2 * NZ), (g // 2) % NZ, g % 2] = t[i * SH:(i + 1) * SH]
    send(ebuf.at[:, :, 1 - mc], ecr, EC, rows=row_of(0, 0, 1))
    s_mid(3)
    give(1, gru.at[0], HALF, ROWS)
    arrived(ecr, EC)

    @pl.loop(0, NX)
    def _(x):
        es[x] = (ebuf[x, :, mc].astype(f32) + ecr[x].astype(f32)).astype(bf)
    for dx in (2, 1, 3):
        send(es.at[lax.rem(mx + dx, NX)], exr.at[mx], EX, rows=row_of(dx, 0, 0))
    exr[mx] = es[mx]
    s_out(3)
    arrived(exr.at[pl.ds(0, NX - 1)], EX)
    for z in range(NZ):
        total = exr[0, z].astype(f32)
        for x in range(1, NX):
            total = total + exr[x, z].astype(f32)
        ez[z] = total.astype(bf)
    for dz in (2, 1, 3):
        send(ez.at[lax.rem(mz + dz, NZ)], ezr.at[mz], EZ, rows=row_of(0, dz, 0))
    ezr[mz] = ez[mz]
    s_wait(3)
    block_grads(2, full.at[3], gru.at[1])
    give(2, gru.at[1], 1, HALF)
    arrived(ezr.at[pl.ds(0, NZ - 1)], EZ)
    total = ezr[0].astype(f32)
    for z in range(1, NZ):
        total = total + ezr[z].astype(f32)
    ishare2 = total.astype(bf)
    ifull[my, ml] = ishare2
    send(ifull.at[my, ml], ifull.at[my, ml], FL, f=feat_of(0, 1))
    give(2, gru.at[1], HALF, ROWS)
    arrived(ifull.at[0, 0], FL)
    y_gather(ifull, FY)
    y_full(ifull, FY)
    block_grads(0, ifull, gri)
    give(0, gri, 1, ROWS)

    arrived(gru.at[0, pl.ds(0, ROWS - 1)], G0 + 1)
    arrived(gru.at[1, pl.ds(0, ROWS - 1)], G0 + 2)
    arrived(gri.at[pl.ds(0, ROWS - 1)], G0)
    for c in unsent:
        c.wait_send()


HALF = ROWS // 2


def accumulate(returned, ids, blocks):
    onehot = (ids.reshape(-1)[:, None] == jnp.arange(blocks, dtype=jnp.int32)[None, :])
    totals = jnp.einsum("prc,pn->rnc", returned.reshape(-1, RP, FBW),
                        onehot.astype(jnp.bfloat16), preferred_element_type=jnp.float32)
    return totals.reshape(RP, blocks * FBW)


def on_device(x_vals, x_blocks, y_vals, y_blocks, user_weights, item_weights, observed, ratings):
    bf, f32 = jnp.bfloat16, jnp.float32
    V = pltpu.VMEM
    n_u, n_i = user_weights.shape[1] // FBW, item_weights.shape[1] // FBW
    slab = (SH, RANK)
    items = (NX, NZ, 2, SH, RANK)
    gru, gri, idx_all = pl.pallas_call(
        kernel,
        out_shape=(jax.ShapeDtypeStruct((2, ROWS, K, RP, FBW), bf),
                   jax.ShapeDtypeStruct((ROWS, K, RP, FBW), bf),
                   jax.ShapeDtypeStruct((ROWS, 4, FBW), jnp.int32)),
        in_specs=[pl.BlockSpec(memory_space=pltpu.VMEM)] * 2
        + [pl.BlockSpec(memory_space=pltpu.SMEM)]
        + [pl.BlockSpec(memory_space=pl.ANY)] * 5,
        out_specs=[pl.BlockSpec(memory_space=pltpu.VMEM)] * 3,
        scratch_shapes=[
            V(user_weights.shape, bf), V(item_weights.shape, bf),
            V((n_u, RP, FBW), bf), V((n_i, RP, FBW), bf),
            V((3 * K, TILE, FBW), bf), V((2 * TILE, ROWS * SH), bf), V((2, ROWS * SH), f32),
            V((4, FBW), jnp.int32), pltpu.SMEM((ROWS, 4, FBW), jnp.int32),
            V((3, ROWS, K, RP, FBW), bf), V((3, ROWS, K, RP, FBW), bf), V((RANK, K * FBW), bf),
            V((NY, 2, *slab), bf), V((NY, 2, *slab), bf), V((2, *slab), bf), V(slab, bf), V(slab, bf),
            V((4, NY, 2, *slab), bf), V((4, NY, 2, *slab), bf), V((4, 2, *slab), bf),
            V((4, 2, *slab), bf), V((4, NY, 2, *slab), bf),
            V(items, bf), V((TILE, ROWS * SH), bf), V((RANK, ROWS * SH), f32),
            V(items, bf), V((NX, NZ, *slab), bf), V((NX, NZ, *slab), bf), V((NX, NZ, *slab), bf),
            V((NZ, *slab), bf), V((NZ, *slab), bf), V((NY, 2, *slab), bf),
            V((3, ROWS, K, RP, FBW), bf), V((RANK, TILE), bf), pltpu.SemaphoreType.DMA((6,)),
            pltpu.SemaphoreType.DMA((NCH,)), pltpu.SemaphoreType.DMA((NCH,)),
        ],
        compiler_params=pltpu.CompilerParams(collective_id=0, has_side_effects=True),
        name="step",
    )(x_blocks.reshape(2, K), y_blocks.reshape(1, K), observed, user_weights, item_weights,
      x_vals.reshape(2 * K, TILE, FBW), y_vals.reshape(K, TILE, FBW),
      ratings.reshape(2 * TILE, ROWS * SH))
    return (accumulate(gru, idx_all[:, 1:3, :K].swapaxes(0, 1), n_u),
            accumulate(gri, idx_all[:, 0, :K], n_i))


def solution(mesh):
    return jax.shard_map(
        on_device,
        mesh=mesh,
        in_specs=(
            P("rows", "feat", None, None, None),
            P("rows", "feat", None),
            P("rows", "feat", None, None, None),
            P("rows", "feat", None),
            P("rows", "feat"),
            P("rows", "feat"),
            P("rows", None),
            P("rows", "feat", None),
        ),
        out_specs=(P("rows", "feat"), P("rows", "feat")),
        check_vma=False,
    )
```

time: 164 us -> 137 us (0.84)
  Pallas kernels: 153 us -> 129 us
  other arithmetic: 2.75 us -> 0 us
  local copies, waits for them, and re-layouts: 6.13 us -> 3.78 us
  matrix products: 0.63 us -> 2.89 us
    pallas_call x1, Pallas kernels: 153 us -> 129 us  [on_device(): pl.pallas_call(kernel, out_shape=(jax.ShapeDtypeStruct((2, ROWS, K, RP, F...]
    dot_general x2, matrix products: 0.63 us -> 2.89 us  [accumulate(): jnp.einsum('prc,pn->rnc', returned.reshape(-1, RP, FBW), onehot.astype(jn...]
where the time goes in v2:
time: 137 us; the launch traced here: 136 us
  Pallas kernels  129 us (94%)
  local copies, waits for them, and re-layouts  3.78 us (3%)
  matrix products  2.89 us (2%)
    pallas_call x1, Pallas kernels, on_device(): pl.pallas_call(kernel, out_shape=(jax.ShapeDtypeStruct((2, ROWS, K, RP, F...  129 us
    dot_general x2, matrix products, accumulate(): jnp.einsum('prc,pn->rnc', returned.reshape(-1, RP, FBW), onehot.astype(jn...  2.89 us

profile of v2, /device:TPU:1, one launch (start us, length us, event | category | flops | bytes accessed | tf_op | source)
XLA Modules:
  0.0 135.9 jit_solution(9136966442238235658)
XLA Ops:
  0.6 128.5 %step.1 = (bf16[2,32,8,8,128]{4,3,2,1,0:T(8,128)(2,1)}, bf16[32,8,8,128]{3,2,1,0:T(8,128)(2,1)}, s32[32,4,128]{2,1,0:T(4,128)}) custom-call(s32[2,8]{1,0:T(2,128)} %bitcast.34, s32[1,8]{1,0:T(1,128)} %bitcast.35, s32[2,32]{1,0:T(2,128)} %observed.1, bf16[8,25088]{1,0:T(8,128)(2,1)} %wu_h.1, bf16[8,12544]{1,0:T(8,128)(2,1)} %wi_h.1, ...), custom_call_target="tpu_custom_call" | custom-call | tf_op jit(solution)/shard_map/step/pallas_call | solution.py:326
  129.2 0.9 slice_reduce_fusion
  130.1 0.9 slice_bitcast_fusion
  130.9 0.1 eq.34
  131.0 1.3 convolution_bitcast_fusion.1
  132.3 0.8 copy.24
  133.1 0.1 eq.30
  133.2 1.6 %convolution_bitcast_fusion = f32[1,8,196,128]{3,2,1,0:T(8,128)S(1)} fusion(bf16[512,8,128]{2,1,0:T(8,128)(2,1)} %bitcast.30, s32[512]{0:T(512)S(1)} %eq.30), kind=kOutput, calls=%fused_computation | convolution fusion | flops 205621248 | bytes 1853440 | tf_op jit(solution)/shard_map/prc,pn->rnc/dot_general | solution.py:315
  134.8 1.0 copy.23
  (1 shorter events, 0.0 us)

commit v3 on v2

--- a/solution.py
+++ b/solution.py
@@ -31,8 +31,8 @@
     return lax.dot_general(a, b, dims, preferred_element_type=jnp.float32)
 
 
-def kernel(x_idx, y_idx, observed, wu_h, wi_h, x_h, y_h, rat_h, gru, gri, idx_all,
-           wu, wi, wu3, wi3, xv, rat, mask, idx_loc, idx_s, asend, arecv, wcat, ipart,
+def kernel(x_idx, y_idx, observed, wu_h, wi_h, x_h, y_h, rat_h, out_u, out_i,
+           gru, gri, idx_all, ohu, ohi, acc, wu, wi, wu3, wi3, xv, rat, mask, idx_loc, idx_s, asend, arecv, wcat, ipart,
            iyr, iys, ilr, ishare, apart, ayr, ays, alr, full, item_all, resid, tacc,
            ebuf, ecr, es, exr, ez, ezr, ifull, gsend, upt, lsem, ssem, rsem):
     row = lax.axis_index("rows")
@@ -213,6 +213,34 @@
             d = row_peer(ROWS - j)
             send(gsend.at[unit, d], out.at[row], G0 + unit, rows=d)
 
+    def onehots():
+        for unit in range(3):
+            ids = idx_all[:, unit]
+            blocks = ohi.shape[0] if unit == 0 else ohu.shape[1]
+            lanes = lax.broadcasted_iota(jnp.int32, (ROWS, blocks), 1)
+            rows = [jnp.where(ids[:, k:k + 1] == lanes, 1.0, 0.0) for k in range(K)]
+            hot = jnp.concatenate(rows, axis=0).T.astype(bf)
+            if unit == 0:
+                ohi[...] = hot
+            else:
+                ohu[unit - 1] = hot
+
+    def accumulate(returned, hot, out, first):
+        for k in range(K):
+            acc[k * RANK:(k + 1) * RANK] = returned[:, k].astype(f32).reshape(RANK, FBW)
+        blocks = out.shape[0] // RP
+        for r in range(0, RP, 2):
+            two = jnp.concatenate(
+                [acc[pl.ds(r + i, ROWS * K, stride=RP)].astype(bf) for i in range(2)], axis=1)
+            o = dot(hot[...], two, NN)
+            for i in range(2):
+                v = o[:blocks, i * FBW:(i + 1) * FBW]
+                at = pl.ds(r + i, blocks, stride=RP)
+                if first:
+                    out[at] = v
+                else:
+                    out[at] += v
+
     ask(0, 1, ROWS)
     ask(1, 1, ROWS)
     for unit in range(3):
@@ -224,7 +252,8 @@
     ask(2, 1, ROWS, sends=False)
     y_sum(iyr, iys, BY)
     send(iys.at[1 - ml], ilr, BL, f=feat_of(0, 1))
-    ask(2, 1, HALF, picks=False)
+    ask(2, 1, 16, picks=False)
+    onehots()
     project(1, apart.at[0])
     s_send(0)
     arrived(ilr, BL)
@@ -232,7 +261,7 @@
     item_all[mx, mz, mc] = ishare[...]
     for dz in (2, 1, 3):
         send(ishare, item_all.at[mx, mz, mc], IZ, rows=row_of(0, dz, 0))
-    ask(2, HALF, ROWS, picks=False)
+    ask(2, 16, ROWS, picks=False)
     s_mid(0)
     arrived(item_all.at[0, pl.ds(0, NZ - 1), 0], IZ)
     for dx in (2, 1, 3):
@@ -255,7 +284,7 @@
     s_send(3)
     s_wait(2)
     block_grads(1, full.at[2], gru.at[0])
-    give(1, gru.at[0], 1, HALF)
+    give(1, gru.at[0], 1, 16)
 
     for q in range(2 * NX):
         t = (tacc[:, q * RANK:(q + 1) * RANK] * grad_scale).T.astype(bf)
@@ -264,7 +293,7 @@
             ebuf[g // (2 * NZ), (g // 2) % NZ, g % 2] = t[i * SH:(i + 1) * SH]
     send(ebuf.at[:, :, 1 - mc], ecr, EC, rows=row_of(0, 0, 1))
     s_mid(3)
-    give(1, gru.at[0], HALF, ROWS)
+    give(1, gru.at[0], 16, ROWS)
     arrived(ecr, EC)
 
     @pl.loop(0, NX)
@@ -285,15 +314,14 @@
     ezr[mz] = ez[mz]
     s_wait(3)
     block_grads(2, full.at[3], gru.at[1])
-    give(2, gru.at[1], 1, HALF)
+    give(2, gru.at[1], 1, 12)
     arrived(ezr.at[pl.ds(0, NZ - 1)], EZ)
     total = ezr[0].astype(f32)
     for z in range(1, NZ):
         total = total + ezr[z].astype(f32)
-    ishare2 = total.astype(bf)
-    ifull[my, ml] = ishare2
+    ifull[my, ml] = total.astype(bf)
     send(ifull.at[my, ml], ifull.at[my, ml], FL, f=feat_of(0, 1))
-    give(2, gru.at[1], HALF, ROWS)
+    give(2, gru.at[1], 12, ROWS)
     arrived(ifull.at[0, 0], FL)
     y_gather(ifull, FY)
     y_full(ifull, FY)
@@ -301,38 +329,33 @@
     give(0, gri, 1, ROWS)
 
     arrived(gru.at[0, pl.ds(0, ROWS - 1)], G0 + 1)
+    accumulate(gru.at[0], ohu.at[0], out_u, True)
     arrived(gru.at[1, pl.ds(0, ROWS - 1)], G0 + 2)
+    accumulate(gru.at[1], ohu.at[1], out_u, False)
     arrived(gri.at[pl.ds(0, ROWS - 1)], G0)
+    accumulate(gri, ohi, out_i, True)
     for c in unsent:
         c.wait_send()
-
-
-HALF = ROWS // 2
-
-
-def accumulate(returned, ids, blocks):
-    onehot = (ids.reshape(-1)[:, None] == jnp.arange(blocks, dtype=jnp.int32)[None, :])
-    totals = jnp.einsum("prc,pn->rnc", returned.reshape(-1, RP, FBW),
-                        onehot.astype(jnp.bfloat16), preferred_element_type=jnp.float32)
-    return totals.reshape(RP, blocks * FBW)
 
 
 def on_device(x_vals, x_blocks, y_vals, y_blocks, user_weights, item_weights, observed, ratings):
     bf, f32 = jnp.bfloat16, jnp.float32
     V = pltpu.VMEM
     n_u, n_i = user_weights.shape[1] // FBW, item_weights.shape[1] // FBW
+    pad_u, pad_i = -(-n_u // FBW) * FBW, -(-n_i // FBW) * FBW
     slab = (SH, RANK)
     items = (NX, NZ, 2, SH, RANK)
-    gru, gri, idx_all = pl.pallas_call(
+    out_u, out_i = pl.pallas_call(
         kernel,
-        out_shape=(jax.ShapeDtypeStruct((2, ROWS, K, RP, FBW), bf),
-                   jax.ShapeDtypeStruct((ROWS, K, RP, FBW), bf),
-                   jax.ShapeDtypeStruct((ROWS, 4, FBW), jnp.int32)),
+        out_shape=(jax.ShapeDtypeStruct((n_u * RP, FBW), f32),
+                   jax.ShapeDtypeStruct((n_i * RP, FBW), f32)),
         in_specs=[pl.BlockSpec(memory_space=pltpu.VMEM)] * 2
         + [pl.BlockSpec(memory_space=pltpu.SMEM)]
         + [pl.BlockSpec(memory_space=pl.ANY)] * 5,
-        out_specs=[pl.BlockSpec(memory_space=pltpu.VMEM)] * 3,
+        out_specs=[pl.BlockSpec(memory_space=pltpu.VMEM)] * 2,
         scratch_shapes=[
+            V((2, ROWS, K, RP, FBW), bf), V((ROWS, K, RP, FBW), bf), V((ROWS, 4, FBW), jnp.int32),
+            V((2, pad_u, ROWS * K), bf), V((pad_i, ROWS * K), bf), V((K * RANK, FBW), f32),
             V(user_weights.shape, bf), V(item_weights.shape, bf),
             V((n_u, RP, FBW), bf), V((n_i, RP, FBW), bf),
             V((3 * K, TILE, FBW), bf), V((2 * TILE, ROWS * SH), bf), V((2, ROWS * SH), f32),
@@ -352,8 +375,8 @@
     )(x_blocks.reshape(2, K), y_blocks.reshape(1, K), observed, user_weights, item_weights,
       x_vals.reshape(2 * K, TILE, FBW), y_vals.reshape(K, TILE, FBW),
       ratings.reshape(2 * TILE, ROWS * SH))
-    return (accumulate(gru, idx_all[:, 1:3, :K].swapaxes(0, 1), n_u),
-            accumulate(gri, idx_all[:, 0, :K], n_i))
+    return (out_u.reshape(n_u, RP, FBW).swapaxes(0, 1).reshape(user_weights.shape),
+            out_i.reshape(n_i, RP, FBW).swapaxes(0, 1).reshape(item_weights.shape))
 
 
 def solution(mesh):

time: 137 us -> 133 us (0.971)
  matrix products: 2.89 us -> 0 us
  Pallas kernels: 129 us -> 127 us
    dot_general x2 -> x0, matrix products: 2.89 us -> none  [accumulate(): jnp.einsum('prc,pn->rnc', returned.reshape(-1, RP, FBW), onehot.astype(jn...]
    unnamed x2, local copies, waits for them, and re-layouts: 1.85 us -> 3.85 us
where the time goes in v3:
time: 133 us; the launch traced here: 132 us
  Pallas kernels  127 us (95%)
  local copies, waits for them, and re-layouts  3.85 us (3%)
    pallas_call x1, Pallas kernels, on_device(): pl.pallas_call(kernel, out_shape=(jax.ShapeDtypeStruct((n_u * RP, FBW), f...  127 us
    unnamed x2, local copies, waits for them, and re-layouts  3.85 us

profile of v3, /device:TPU:1, one launch (start us, length us, event | category | flops | bytes accessed | tf_op | source)
XLA Modules:
  0.0 131.7 jit_solution(8909824960784160159)
XLA Ops:
  0.6 127.2 %step.1 = (f32[1568,128]{1,0:T(8,128)}, f32[784,128]{1,0:T(8,128)}) custom-call(s32[2,8]{1,0:T(2,128)} %bitcast.20, s32[1,8]{1,0:T(1,128)} %bitcast.21, s32[2,32]{1,0:T(2,128)} %observed.1, bf16[8,25088]{1,0:T(8,128)(2,1)} %wu_h.1, bf16[8,12544]{1,0:T(8,128)(2,1)} %wi_h.1, bf16[16,512,128]{2,1,0:T(8,128)(2,1)} %bitcast.16, bf16[8,512,128]{2,1,0:T(8,128)(2,1)} %bitcast.17, ...), custom_call_target="tpu_custom_call" | custom-call | tf_op jit(solution)/shard_map/step/pallas_call | solution.py:348
  127.8 2.1 %copy.12 = f32[8,25088]{1,0:T(8,128)} copy(f32[8,25088]{1,0:T(8,128)} %bitcast.18) | data formatting | bytes 1605632
  129.9 1.8 %copy.13 = f32[8,12544]{1,0:T(8,128)} copy(f32[8,12544]{1,0:T(8,128)} %bitcast.19) | data formatting | bytes 802816

commit v4 on v3

--- a/solution.py
+++ b/solution.py
@@ -19,6 +19,7 @@
 NY = FEAT // 2
 RP = RANK // ROWS
 MESH = pl.DeviceIdType.MESH
+DIRECT = (1, 2)
 
 IDX, A0, BY, BL, IZ, IX, IC, EC, EX, EZ, FL, FY, G0, UY, UL, UG, NCH = (
     0, 1, 4, 5, 6, 7, 8, 9, 10, 11, 12, 13, 14, 17, 21, 25, 29)
@@ -78,7 +79,7 @@
     def _(j):
         pl.semaphore_signal(barrier, inc=1, device_id={"rows": row_peer(ROWS - j), "feat": feat},
                             device_id_type=MESH)
-    feat_peers = [(0, 1)] + [(dy, 0) for dy in (2, 1, 3)]
+    feat_peers = [(dy, dl) for dy in (2, 1, 3) for dl in (1, 0)] + [(0, 1)]
     for dy, dl in feat_peers:
         pl.semaphore_signal(barrier, inc=1, device_id={"rows": row, "feat": feat_of(dy, dl)},
                             device_id_type=MESH)
@@ -139,43 +140,62 @@
             xt = jnp.concatenate(
                 [xv[unit * K + k, h * half:(h + 1) * half] for k in range(K)], axis=1)
             p = dot(xt, wcat[...], NT)
-            dst[h * 2:(h + 1) * 2] = p.astype(bf).reshape(2, 2, SH, RANK)
+            dst[h * 4:(h + 1) * 4] = p.astype(bf).reshape(4, SH, RANK)
+
+    def quarter(y):
+        return pl.ds(2 * y, 2)
 
     def y_scatter(src, dst, ch):
         for dy in (2, 1, 3):
             y = lax.rem(my + dy, NY)
-            send(src.at[y], dst.at[my], ch, f=feat_of(dy, 0))
-        dst[my] = src[my]
+            send(src.at[quarter(y)], dst.at[quarter(my)], ch, f=feat_of(dy, 0))
+        dst[quarter(my)] = src[quarter(my)]
 
     def y_sum(dst, out, ch):
-        arrived(dst.at[pl.ds(0, NY - 1)], ch)
+        arrived(dst.at[pl.ds(0, FEAT - 2)], ch)
         for l in range(2):
-            total = dst[0, l].astype(f32)
+            total = dst[l].astype(f32)
             for y in range(1, NY):
-                total = total + dst[y, l].astype(f32)
+                total = total + dst[2 * y + l].astype(f32)
             out[l] = total.astype(bf)
 
     def y_gather(dst, ch):
         for dy in (2, 1, 3):
-            send(dst.at[my], dst.at[my], ch, f=feat_of(dy, 0))
+            send(dst.at[quarter(my)], dst.at[quarter(my)], ch, f=feat_of(dy, 0))
 
     def y_full(dst, ch):
-        arrived(dst.at[pl.ds(0, NY - 1)], ch)
+        arrived(dst.at[pl.ds(0, FEAT - 2)], ch)
 
     def s_send(i):
-        y_scatter(apart.at[i], ayr.at[i], UY + i)
+        if i not in DIRECT:
+            y_scatter(apart.at[i], ayr.at[i], UY + i)
+            return
+        for dy, dl in feat_peers:
+            f = feat_of(dy, dl)
+            send(apart.at[i, f], ayr.at[i, feat], UY + i, f=f)
+        ayr[i, feat] = apart[i, feat]
 
     def s_mid(i):
-        y_sum(ayr.at[i], ays.at[i], UY + i)
-        send(ays.at[i], alr.at[i], UL + i, f=feat_of(0, 1))
+        if i not in DIRECT:
+            y_sum(ayr.at[i], ays.at[i], UY + i)
+            send(ays.at[i], alr.at[i], UL + i, f=feat_of(0, 1))
+            return
+        arrived(ayr.at[i, pl.ds(0, FEAT - 1)], UY + i)
+        total = ayr[i, 0].astype(f32)
+        for f in range(1, FEAT):
+            total = total + ayr[i, f].astype(f32)
+        full[i, feat] = total.astype(bf)
+        for dy, dl in feat_peers:
+            send(full.at[i, feat], full.at[i, feat], UG + i, f=feat_of(dy, dl))
 
     def s_out(i):
-        arrived(alr.at[i], UL + i)
-        full[i, my] = (ays[i].astype(f32) + alr[i].astype(f32)).astype(bf)
-        y_gather(full.at[i], UG + i)
+        if i not in DIRECT:
+            arrived(alr.at[i], UL + i)
+            full[i, quarter(my)] = (ays[i].astype(f32) + alr[i].astype(f32)).astype(bf)
+            y_gather(full.at[i], UG + i)
 
     def s_wait(i):
-        y_full(full.at[i], UG + i)
+        arrived(full.at[i, pl.ds(0, FEAT - (1 if i in DIRECT else 2))], UG + i)
 
     def residual(b):
         upt[...] = full[b].reshape(TILE, RANK).T
@@ -195,7 +215,7 @@
                 tacc[:, cols] += t
         for h in range(2):
             g = dot(resid[h * RANK:(h + 1) * RANK, :], item_all[...].reshape(ROWS * SH, RANK), NN)
-            apart[2 + b, h * 2:(h + 1) * 2] = (g * grad_scale).astype(bf).reshape(2, 2, SH, RANK)
+            apart[2 + b, h * 4:(h + 1) * 4] = (g * grad_scale).astype(bf).reshape(4, SH, RANK)
 
     def block_grads(unit, src, out):
         gt = src[...].reshape(TILE, RANK).T
@@ -242,7 +262,8 @@
                     out[at] += v
 
     ask(0, 1, ROWS)
-    ask(1, 1, ROWS)
+    ask(1, 1, 24)
+    ask(1, 24, ROWS, sends=False)
     for unit in range(3):
         pick(unit, arecv.at[unit, row], row)
     for c in loads[2:]:
@@ -252,7 +273,7 @@
     ask(2, 1, ROWS, sends=False)
     y_sum(iyr, iys, BY)
     send(iys.at[1 - ml], ilr, BL, f=feat_of(0, 1))
-    ask(2, 1, 16, picks=False)
+    ask(1, 24, ROWS, picks=False)
     onehots()
     project(1, apart.at[0])
     s_send(0)
@@ -261,8 +282,9 @@
     item_all[mx, mz, mc] = ishare[...]
     for dz in (2, 1, 3):
         send(ishare, item_all.at[mx, mz, mc], IZ, rows=row_of(0, dz, 0))
-    ask(2, 16, ROWS, picks=False)
+    ask(2, 1, 17, picks=False)
     s_mid(0)
+    ask(2, 17, ROWS, picks=False)
     arrived(item_all.at[0, pl.ds(0, NZ - 1), 0], IZ)
     for dx in (2, 1, 3):
         send(item_all.at[mx, :, mc], item_all.at[mx, :, mc], IX, rows=row_of(dx, 0, 0))
@@ -319,10 +341,10 @@
     total = ezr[0].astype(f32)
     for z in range(1, NZ):
         total = total + ezr[z].astype(f32)
-    ifull[my, ml] = total.astype(bf)
-    send(ifull.at[my, ml], ifull.at[my, ml], FL, f=feat_of(0, 1))
+    ifull[feat] = total.astype(bf)
+    send(ifull.at[feat], ifull.at[feat], FL, f=feat_of(0, 1))
     give(2, gru.at[1], 12, ROWS)
-    arrived(ifull.at[0, 0], FL)
+    arrived(ifull.at[0], FL)
     y_gather(ifull, FY)
     y_full(ifull, FY)
     block_grads(0, ifull, gri)
@@ -361,12 +383,12 @@
             V((3 * K, TILE, FBW), bf), V((2 * TILE, ROWS * SH), bf), V((2, ROWS * SH), f32),
             V((4, FBW), jnp.int32), pltpu.SMEM((ROWS, 4, FBW), jnp.int32),
             V((3, ROWS, K, RP, FBW), bf), V((3, ROWS, K, RP, FBW), bf), V((RANK, K * FBW), bf),
-            V((NY, 2, *slab), bf), V((NY, 2, *slab), bf), V((2, *slab), bf), V(slab, bf), V(slab, bf),
-            V((4, NY, 2, *slab), bf), V((4, NY, 2, *slab), bf), V((4, 2, *slab), bf),
-            V((4, 2, *slab), bf), V((4, NY, 2, *slab), bf),
+            V((FEAT, *slab), bf), V((FEAT, *slab), bf), V((2, *slab), bf), V(slab, bf), V(slab, bf),
+            V((4, FEAT, *slab), bf), V((4, FEAT, *slab), bf), V((4, 2, *slab), bf),
+            V((4, 2, *slab), bf), V((4, FEAT, *slab), bf),
             V(items, bf), V((TILE, ROWS * SH), bf), V((RANK, ROWS * SH), f32),
             V(items, bf), V((NX, NZ, *slab), bf), V((NX, NZ, *slab), bf), V((NX, NZ, *slab), bf),
-            V((NZ, *slab), bf), V((NZ, *slab), bf), V((NY, 2, *slab), bf),
+            V((NZ, *slab), bf), V((NZ, *slab), bf), V((FEAT, *slab), bf),
             V((3, ROWS, K, RP, FBW), bf), V((RANK, TILE), bf), pltpu.SemaphoreType.DMA((6,)),
             pltpu.SemaphoreType.DMA((NCH,)), pltpu.SemaphoreType.DMA((NCH,)),
         ],

time: 133 us -> 132 us (level)
  no operation moved by 1% of the time
where the time goes in v4:
time: 132 us
  Pallas kernels  127 us (96%)
  local copies, waits for them, and re-layouts  3.85 us (3%)
    pallas_call x1, Pallas kernels, on_device(): pl.pallas_call(kernel, out_shape=(jax.ShapeDtypeStruct((n_u * RP, FBW), f...  127 us
    unnamed x2, local copies, waits for them, and re-layouts  3.85 us

profile of v4, /device:TPU:1, one launch (start us, length us, event | category | flops | bytes accessed | tf_op | source)
XLA Modules:
  0.0 131.9 jit_solution(854416370915599604)
XLA Ops:
  0.6 127.4 %step.1 = (f32[1568,128]{1,0:T(8,128)}, f32[784,128]{1,0:T(8,128)}) custom-call(s32[2,8]{1,0:T(2,128)} %bitcast.20, s32[1,8]{1,0:T(1,128)} %bitcast.21, s32[2,32]{1,0:T(2,128)} %observed.1, bf16[8,25088]{1,0:T(8,128)(2,1)} %wu_h.1, bf16[8,12544]{1,0:T(8,128)(2,1)} %wi_h.1, bf16[16,512,128]{2,1,0:T(8,128)(2,1)} %bitcast.16, bf16[8,512,128]{2,1,0:T(8,128)(2,1)} %bitcast.17, ...), custom_call_target="tpu_custom_call" | custom-call | tf_op jit(solution)/shard_map/step/pallas_call | solution.py:370
  128.0 2.1 %copy.12 = f32[8,25088]{1,0:T(8,128)} copy(f32[8,25088]{1,0:T(8,128)} %bitcast.18) | data formatting | bytes 1605632
  130.1 1.8 %copy.13 = f32[8,12544]{1,0:T(8,128)} copy(f32[8,12544]{1,0:T(8,128)} %bitcast.19) | data formatting | bytes 802816

commit v5 on v4

--- a/solution.py
+++ b/solution.py
@@ -21,8 +21,8 @@
 MESH = pl.DeviceIdType.MESH
 DIRECT = (1, 2)
 
-IDX, A0, BY, BL, IZ, IX, IC, EC, EX, EZ, FL, FY, G0, UY, UL, UG, NCH = (
-    0, 1, 4, 5, 6, 7, 8, 9, 10, 11, 12, 13, 14, 17, 21, 25, 29)
+IDX, A0, BY, BL, IZ, IX, IC, EX, EZ, FL, FY, G0, UY, UL, UG, EC, NCH = (
+    0, 1, 4, 5, 6, 7, 8, 9, 10, 11, 12, 13, 16, 20, 24, 28, 32)
 
 NT = (((1,), (1,)), ((), ()))
 NN = (((1,), (0,)), ((), ()))
@@ -308,22 +308,25 @@
     block_grads(1, full.at[2], gru.at[0])
     give(1, gru.at[0], 1, 16)
 
-    for q in range(2 * NX):
-        t = (tacc[:, q * RANK:(q + 1) * RANK] * grad_scale).T.astype(bf)
-        for i in range(4):
-            g = q * 4 + i
-            ebuf[g // (2 * NZ), (g // 2) % NZ, g % 2] = t[i * SH:(i + 1) * SH]
-    send(ebuf.at[:, :, 1 - mc], ecr, EC, rows=row_of(0, 0, 1))
+    for dx in (2, 1, 3, 0):
+        x = lax.rem(mx + dx, NX)
+        for h in range(2):
+            cols = pl.ds(pl.multiple_of(x * TILE + h * RANK, RANK), RANK)
+            t = (tacc[:, cols] * grad_scale).T.astype(bf)
+            for i in range(4):
+                ebuf[x, h * 2 + i // 2, i % 2] = t[i * SH:(i + 1) * SH]
+        send(ebuf.at[x, :, 1 - mc], ecr.at[x], EC + dx, rows=row_of(0, 0, 1))
     s_mid(3)
     give(1, gru.at[0], 16, ROWS)
-    arrived(ecr, EC)
-
-    @pl.loop(0, NX)
-    def _(x):
-        es[x] = (ebuf[x, :, mc].astype(f32) + ecr[x].astype(f32)).astype(bf)
-    for dx in (2, 1, 3):
-        send(es.at[lax.rem(mx + dx, NX)], exr.at[mx], EX, rows=row_of(dx, 0, 0))
-    exr[mx] = es[mx]
+    for dx in (2, 1, 3, 0):
+        x = lax.rem(mx + dx, NX)
+        arrived(ecr.at[0], EC + dx)
+        both = (ebuf[x, :, mc].astype(f32) + ecr[x].astype(f32)).astype(bf)
+        if dx:
+            es[x] = both
+            send(es.at[x], exr.at[mx], EX, rows=row_of(dx, 0, 0))
+        else:
+            exr[mx] = both
     s_out(3)
     arrived(exr.at[pl.ds(0, NX - 1)], EX)
     for z in range(NZ):

time: 132 us -> 131 us (level)
  no operation moved by 1% of the time
where the time goes in v5:
time: 131 us
  Pallas kernels  127 us (97%)
  local copies, waits for them, and re-layouts  3.85 us (3%)
    pallas_call x1, Pallas kernels, on_device(): pl.pallas_call(kernel, out_shape=(jax.ShapeDtypeStruct((n_u * RP, FBW), f...  127 us
    unnamed x2, local copies, waits for them, and re-layouts  3.85 us

profile of v5, /device:TPU:1, one launch (start us, length us, event | category | flops | bytes accessed | tf_op | source)
XLA Modules:
  0.0 131.2 jit_solution(13989433361975260100)
XLA Ops:
  0.6 126.7 %step.1 = (f32[1568,128]{1,0:T(8,128)}, f32[784,128]{1,0:T(8,128)}) custom-call(s32[2,8]{1,0:T(2,128)} %bitcast.20, s32[1,8]{1,0:T(1,128)} %bitcast.21, s32[2,32]{1,0:T(2,128)} %observed.1, bf16[8,25088]{1,0:T(8,128)(2,1)} %wu_h.1, bf16[8,12544]{1,0:T(8,128)(2,1)} %wi_h.1, bf16[16,512,128]{2,1,0:T(8,128)(2,1)} %bitcast.16, bf16[8,512,128]{2,1,0:T(8,128)(2,1)} %bitcast.17, ...), custom_call_target="tpu_custom_call" | custom-call | tf_op jit(solution)/shard_map/step/pallas_call | solution.py:373
  127.4 2.1 %copy.12 = f32[8,25088]{1,0:T(8,128)} copy(f32[8,25088]{1,0:T(8,128)} %bitcast.18) | data formatting | bytes 1605632
  129.4 1.8 %copy.13 = f32[8,12544]{1,0:T(8,128)} copy(f32[8,12544]{1,0:T(8,128)} %bitcast.19) | data formatting | bytes 802816
